TPU v7x, 512 devices: a whole 4x4x16 slice. The times are simulated.
512 devices in a mesh: rows: 128 (over z, x, core), grp: 4 (over y).
Axes of the slice: x: 4, y: 4, z: 16, core: 2. Of those that a mesh axis runs over, the one named last changes fastest.
Arguments:
- features: bfloat16 [4, 196608, 128], P('grp', 'rows'), may hold values from -6 to 6
- length_scale: bfloat16 [4, 196608], P('grp', 'rows'), may hold values from 32 to 256
- prior: bfloat16 [4, 196608], P('grp', 'rows'), may hold values from 0.45 to 18
- partners: int32 [4, 1536, 16], P('grp', 'rows'), may hold values from 0 to 1535, as said below
- counts: int32 [4, 1536], P('grp', 'rows'), may hold values from 12 to 16
- projection: bfloat16 [128, 64], replicated, may hold values from -0.5 to 0.5
Outputs:
- first_basis: float32 [4, 64, 196608], P('grp', None, 'rows')
- embedding: float32 [4, 64, 196608], P('grp', None, 'rows')
Inputs may be any that keep to these rules, and one draw needn't show every extreme that they name: `partners`: slot 0 of each tile names the tile itself; slots 1 to 12 name tiles held by the same device; slots 13 onward name tiles held by other devices along rows in the same group. Tiles may repeat in a list. Over one device's tiles, slots 13 onward name tiles of any one other device at most 1 times, and exactly 1 times for some device.
All inputs are finite; a program needn't handle non-finite values.
Results may differ from a plain program's by a relative error of at most 0.0047.
Values may be sent and summed in bfloat16 or wider, within the bound.
A program may use at most 128 MiB of HBM per device.

v0:
```python
import jax
import jax.numpy as jnp
from jax import lax
from jax.sharding import PartitionSpec as P

NEAR = 13


def kernel_tiles(own_rows, own_norm, own_band, part_rows, part_norm, part_band, alive_mask):
    cross_products = jnp.einsum(
        "naf,nsbf->nsab", own_rows, part_rows, preferred_element_type=jnp.float32
    )
    distance = jnp.maximum(
        own_norm[:, None, :, None] + part_norm[:, :, None, :] - 2.0 * cross_products, 0.0
    )
    spread = (
        own_band.astype(jnp.float32)[:, None, :, None]
        + part_band.astype(jnp.float32)[:, :, None, :]
    )
    return jnp.where(alive_mask[:, :, None, None], jnp.exp(-distance / spread), 0.0)


def density_term(kernel, extras):
    return jnp.sum(kernel, axis=(1, 3))


def walk_term(kernel, extras):
    rounded = lax.optimization_barrier(kernel.astype(jnp.bfloat16))
    degree = jnp.sum(rounded.astype(jnp.float32) * extras[0][:, :, None, :], axis=(1, 3))
    product = jnp.einsum("nsab,nscb->nca", rounded, extras[1], preferred_element_type=jnp.float32)
    return (degree, product)


def apply_term(kernel, extras):
    rounded = kernel.astype(jnp.bfloat16)
    return jnp.einsum("nsab,nscb->nca", rounded, extras[0], preferred_element_type=jnp.float32)


def sweep_blocks(block_term, own_arrays, pool_arrays, slot_table, alive_table, block_size):
    tiles_dev = own_arrays[0].shape[0]

    def one_block(block_step):
        first_tile = block_step * block_size
        own_block = [
            lax.dynamic_slice_in_dim(member, first_tile, block_size, 0) for member in own_arrays
        ]
        slot_block = lax.dynamic_slice_in_dim(slot_table, first_tile, block_size, 0)
        alive_block = lax.dynamic_slice_in_dim(alive_table, first_tile, block_size, 0)
        gathered = [jnp.take(member, slot_block, axis=0) for member in pool_arrays]
        kernel = kernel_tiles(
            own_block[0],
            own_block[1],
            own_block[2],
            gathered[0],
            gathered[1],
            gathered[2],
            alive_block,
        )
        return block_term(kernel, gathered[3:])

    stacked = lax.map(one_block, jnp.arange(tiles_dev // block_size, dtype=jnp.int32))
    return jax.tree.map(
        lambda stacked_part: stacked_part.reshape((tiles_dev,) + stacked_part.shape[2:]), stacked
    )


def combined(
    block_term,
    own_arrays,
    near_extras,
    far_arrays,
    far_extras,
    near_table,
    far_table,
    alive_table,
    block_size,
):
    pool_arrays = tuple(
        (
            jnp.concatenate([near_member, far_member], axis=0)
            for near_member, far_member in zip(own_arrays + near_extras, far_arrays + far_extras)
        )
    )
    slot_table = jnp.concatenate([near_table, far_table + own_arrays[0].shape[0]], axis=1)
    return sweep_blocks(block_term, own_arrays, pool_arrays, slot_table, alive_table, block_size)


def orthonormal(raw_basis, total_rows):
    local_gram = jnp.einsum("nca,nda->cd", raw_basis, raw_basis, precision=lax.Precision.HIGHEST)
    gram_matrix = lax.psum(local_gram, ("rows", "grp")) / total_rows
    lower = jnp.linalg.cholesky(gram_matrix)
    identity = jnp.eye(gram_matrix.shape[0], dtype=jnp.float32)
    lower_inverse = lax.linalg.triangular_solve(lower, identity, left_side=True, lower=True)
    return jnp.einsum("dc,nca->nda", lower_inverse, raw_basis, precision=lax.Precision.HIGHEST)


def columns_first(tile_basis):
    return jnp.transpose(tile_basis, (1, 0, 2)).reshape(
        1, tile_basis.shape[1], tile_basis.shape[0] * tile_basis.shape[2]
    )


def shards(features, length_scale, prior, partners, counts, projection):
    tiles_dev = partners.shape[1]
    part_slots = partners.shape[2]
    tile_rows = features.shape[1] // tiles_dev
    feature_width = features.shape[2]
    column_count = projection.shape[1]
    nrows = lax.axis_size("rows")
    device_index = lax.axis_index("rows")
    own_rows = features[0].reshape(tiles_dev, tile_rows, feature_width)
    own_band = length_scale[0].reshape(tiles_dev, tile_rows)
    own_prior = prior[0].reshape(tiles_dev, tile_rows)
    own_norm = jnp.einsum("naf,naf->na", own_rows, own_rows, preferred_element_type=jnp.float32)
    partner_lists = partners[0]
    far_tiles = partner_lists[:, NEAR:].reshape(-1)
    far_count = far_tiles.shape[0]
    capacity = max(1, (3 * far_count + 2 * nrows - 3) // (2 * (nrows - 1)))
    near_table = partner_lists[:, :NEAR] - device_index * tiles_dev
    alive_table = jnp.arange(part_slots, dtype=jnp.int32)[None, :] < counts[0][:, None]
    block_size = 2
    owner_index = far_tiles // tiles_dev
    local_index = far_tiles % tiles_dev
    owner_hits = (owner_index[:, None] == jnp.arange(nrows, dtype=jnp.int32)[None, :]).astype(
        jnp.int32
    )
    slot_rank = jnp.sum((jnp.cumsum(owner_hits, axis=0) - owner_hits) * owner_hits, axis=1)
    wanted = jnp.zeros((nrows, capacity), jnp.int32).at[owner_index, slot_rank].set(local_index)
    requested = lax.all_to_all(wanted, "rows", split_axis=0, concat_axis=0, tiled=True)
    got_rows, got_band, got_prior = (
        lax.all_to_all(
            jnp.take(own_rows, requested, axis=0), "rows", split_axis=0, concat_axis=0, tiled=True
        ),
        lax.all_to_all(
            jnp.take(own_band, requested, axis=0), "rows", split_axis=0, concat_axis=0, tiled=True
        ),
        lax.all_to_all(
            jnp.take(own_prior, requested, axis=0), "rows", split_axis=0, concat_axis=0, tiled=True
        ),
    )
    far_rows = got_rows.reshape(nrows * capacity, tile_rows, feature_width)
    far_band = got_band.reshape(nrows * capacity, tile_rows)
    far_prior = got_prior.reshape(nrows * capacity, tile_rows)
    far_table = (owner_index * capacity + slot_rank).reshape(tiles_dev, part_slots - NEAR)
    far_norm = jnp.einsum("naf,naf->na", far_rows, far_rows, preferred_element_type=jnp.float32)
    own_arrays = (own_rows, own_norm, own_band)
    far_arrays = (far_rows, far_norm, far_band)
    density = combined(
        density_term, own_arrays, (), far_arrays, (), near_table, far_table, alive_table, block_size
    )
    own_inverse = 1.0 / density
    far_inverse = (
        lax.all_to_all(
            jnp.take(own_inverse, requested, axis=0).astype(jnp.bfloat16),
            "rows",
            split_axis=0,
            concat_axis=0,
            tiled=True,
        )
        .astype(jnp.float32)
        .reshape(nrows * capacity, tile_rows)
    )
    own_start = jnp.einsum("naf,fc->nca", own_rows, projection, preferred_element_type=jnp.float32)
    own_scaled = (own_start * (own_prior.astype(jnp.float32) * own_inverse)[:, None, :]).astype(
        jnp.bfloat16
    )
    far_start = jnp.einsum("naf,fc->nca", far_rows, projection, preferred_element_type=jnp.float32)
    far_scaled = (far_start * (far_prior.astype(jnp.float32) * far_inverse)[:, None, :]).astype(
        jnp.bfloat16
    )
    degree, product = combined(
        walk_term,
        own_arrays,
        (own_inverse, own_scaled),
        far_arrays,
        (far_inverse, far_scaled),
        near_table,
        far_table,
        alive_table,
        block_size,
    )
    total_rows = nrows * lax.axis_size("grp") * tiles_dev * tile_rows
    first_basis = orthonormal(product / degree[:, None, :], total_rows)
    own_next = (first_basis * own_inverse[:, None, :]).astype(jnp.bfloat16)
    far_next = lax.all_to_all(
        jnp.take(own_next, requested, axis=0), "rows", split_axis=0, concat_axis=0, tiled=True
    ).reshape(nrows * capacity, column_count, tile_rows)
    second = combined(
        apply_term,
        own_arrays,
        (own_next,),
        far_arrays,
        (far_next,),
        near_table,
        far_table,
        alive_table,
        block_size,
    )
    final_basis = orthonormal(second / degree[:, None, :], total_rows)
    return (columns_first(first_basis), columns_first(final_basis))


def solution(mesh):
    in_specs = (
        P("grp", "rows", None),
        P("grp", "rows"),
        P("grp", "rows"),
        P("grp", "rows", None),
        P("grp", "rows"),
        P(),
    )
    out_specs = (P("grp", None, "rows"), P("grp", None, "rows"))
    return jax.shard_map(shards, mesh=mesh, in_specs=in_specs, out_specs=out_specs, check_vma=False)
```

profile of v0, /device:TPU:1, one launch (start us, length us, event | category | flops | bytes accessed | tf_op | source)
XLA Modules:
  0.0 839.4 jit_solution(2037871099502354747)
XLA Ops:
  4.0 20.4 %all-to-all-start = ((s32[128,1,1]{2,1,0:T(1,128)}), s32[128,1,1]{2,1,0:T(1,128)S(1)}, u32[]{:S(2)}, u32[]{:S(2)}) async-start(s32[128,1,1]{2,1,0:T(1,128)} %copy.68), calls=%async_computation | async-start | bytes 131072 | tf_op jit(solution)/shard_map/all_to_all | solution.py:129
  25.8 13.4 %all-to-all-done = s32[128,1,1]{2,1,0:T(1,128)S(1)} async-done(((s32[128,1,1]{2,1,0:T(1,128)}), s32[128,1,1]{2,1,0:T(1,128)S(1)}, u32[]{:S(2)}, u32[]{:S(2)}) %all-to-all-start) | async-done | bytes 544 | tf_op jit(solution)/shard_map/all_to_all | solution.py:129
  39.2 2.3 reduce.9
  41.6 2.4 and_reduce_fusion
  43.9 2.4 reduce.7
  48.5 5.6 all-to-all-start.2
  54.2 3.0 gather_fusion.12
  57.2 4.6 fusion.70
  61.7 7.5 all-to-all-done.2
  69.2 9.3 %all-to-all-start.1 = ((bf16[128,1,128,128]{3,2,1,0:T(8,128)(2,1)}), bf16[128,1,128,128]{3,2,1,0:T(8,128)(2,1)}, u32[]{:S(2)}, u32[]{:S(2)}) async-start(bf16[128,1,128,128]{3,2,1,0:T(8,128)(2,1)} %fusion.70), calls=%async_computation.1 | async-start | bytes 8388608 | tf_op jit(solution)/shard_map/all_to_all | solution.py:131
  79.7 182.3 %all-to-all-done.1 = bf16[128,1,128,128]{3,2,1,0:T(8,128)(2,1)} async-done(((bf16[128,1,128,128]{3,2,1,0:T(8,128)(2,1)}), bf16[128,1,128,128]{3,2,1,0:T(8,128)(2,1)}, u32[]{:S(2)}, u32[]{:S(2)}) %all-to-all-start.1) | async-done | bytes 4194336 | tf_op jit(solution)/shard_map/all_to_all | solution.py:131
  262.1 4.6 pad_maximum_fusion
  266.7 4.4 fusion.69
  271.2 45.2 %while.32 = (s32[]{:T(128)}, f32[6,2,128]{2,1,0:T(2,128)S(1)}, s32[6]{0:T(128)S(1)}, pred[12,16]{1,0:T(8,128)(4,1)S(1)}, f32[12,128]{1,0:T(8,128)S(1)}, /*index=...) while((s32[]{:T(128)}, f32[6,2,128]{2,1,0:T(2,128)S(1)}, ...), condition=%wide.region_5.10_spmd, body=%wide.region_3.9_spmd.sunk | while | flops 139474112 | bytes 3365755 | solution.py:61
  273.8 3.0 gather_fusion
  281.3 3.0 gather_fusion
  288.8 3.0 gather_fusion
  296.4 3.0 gather_fusion
  303.9 3.0 gather_fusion
  311.4 3.0 gather_fusion
  317.8 13.1 %all-to-all-start.3 = ((bf16[128,1,128]{2,1,0:T(2,128)(2,1)}), bf16[128,1,128]{2,1,0:T(2,128)(2,1)S(1)}, u32[]{:S(2)}, u32[]{:S(2)}) async-start(bf16[128,1,128]{2,1,0:T(2,128)(2,1)} %copy.71), calls=%async_computation.3 | async-start | bytes 131072 | tf_op jit(solution)/shard_map/all_to_all | solution.py:153
  330.9 14.8 %all-to-all-done.3 = bf16[128,1,128]{2,1,0:T(2,128)(2,1)S(1)} async-done(((bf16[128,1,128]{2,1,0:T(2,128)(2,1)}), bf16[128,1,128]{2,1,0:T(2,128)(2,1)S(1)}, u32[]{:S(2)}, u32[]{:S(2)}) %all-to-all-start.3) | async-done | bytes 32800 | tf_op jit(solution)/shard_map/all_to_all | solution.py:153
  345.7 5.9 all-to-all-start.4
  352.1 14.5 %all-to-all-done.4 = bf16[128,1,128]{2,1,0:T(2,128)(2,1)S(1)} async-done(((bf16[128,1,128]{2,1,0:T(2,128)(2,1)}), bf16[128,1,128]{2,1,0:T(2,128)(2,1)S(1)}, u32[]{:S(2)}, u32[]{:S(2)}) %all-to-all-start.4) | async-done | bytes 32800 | tf_op jit(solution)/shard_map/all_to_all | solution.py:137
  366.6 3.8 fusion.72
  372.1 69.3 %while.33 = (s32[]{:T(128)}, f32[6,2,128]{2,1,0:T(2,128)S(1)}, f32[6,2,64,128]{3,2,1,0:T(8,128)S(1)}, s32[6]{0:T(128)S(1)}, pred[12,16]{1,0:T(8,128)(4,1)S(1)}, ...) while((s32[]{:T(128)}, f32[6,2,128]{2,1,0:T(2,128)S(1)}, ...), condition=%wide.region_8.14_spmd, body=%wide.region_6.13_spmd.sunk | while | flops 208422080 | bytes 8232599 | solution.py:61
  375.3 3.0 gather_fusion.3
  380.2 2.3 gather_fusion.7
  386.9 3.0 gather_fusion.3
  398.4 3.0 gather_fusion.3
  410.0 3.0 gather_fusion.3
  421.5 3.0 gather_fusion.3
  433.1 3.0 gather_fusion.3
  441.9 100.7 %psum.14 = f32[64,64]{0,1:T(8,128)S(1)} all-reduce(f32[64,64]{0,1:T(8,128)S(1)} %convolution_bitcast_fusion.4), channel_id=1, replica_groups=mesh['rows'=128,'grp'=4] {'rows','grp'}, use_global_device_ids=true, to_apply=%region_9.15 | all-reduce | flops 4096 | bytes 32768 | tf_op jit(solution)/shard_map/psum | solution.py:90
  542.7 5.8 cholesky.44
  549.9 4.9 custom-call.6
  558.1 9.4 %all-to-all-start.5 = ((bf16[128,1,64,128]{3,2,1,0:T(8,128)(2,1)}), bf16[128,1,64,128]{3,2,1,0:T(8,128)(2,1)S(1)}, u32[]{:S(2)}, u32[]{:S(2)}) async-start(bf16[128,1,64,128]{3,2,1,0:T(8,128)(2,1)} %fusion.71), calls=%async_computation.5 | async-start | bytes 4194304 | tf_op jit(solution)/shard_map/all_to_all | solution.py:185
  570.5 93.9 %all-to-all-done.5 = bf16[128,1,64,128]{3,2,1,0:T(8,128)(2,1)S(1)} async-done(((bf16[128,1,64,128]{3,2,1,0:T(8,128)(2,1)}), bf16[128,1,64,128]{3,2,1,0:T(8,128)(2,1)S(1)}, u32[]{:S(2)}, u32[]{:S(2)}) %all-to-all-start.5) | async-done | bytes 2097184 | tf_op jit(solution)/shard_map/all_to_all | solution.py:185
  666.0 57.1 %while.34 = (s32[]{:T(128)}, f32[6,2,64,128]{3,2,1,0:T(8,128)S(1)}, s32[6]{0:T(128)S(1)}, s32[12,16]{1,0:T(8,128)S(1)}, bf16[140,64,128]{2,1,0:T(8,128)(2,1)}, /...) while((s32[]{:T(128)}, f32[6,2,64,128]{3,2,1,0:T(8,128)S(1)}, ...), condition=%wide.region_13.21_spmd, body=%wide.region_12.20_spmd.sunk | while | flops 206845376 | bytes 5001731 | solution.py:61
  668.6 3.0 gather_fusion.8
  678.1 3.0 gather_fusion.8
  687.6 3.0 gather_fusion.8
  697.1 3.0 gather_fusion.8
  706.7 3.0 gather_fusion.8
  716.2 3.0 gather_fusion.8
  723.6 101.9 %psum.15 = f32[64,64]{0,1:T(8,128)S(1)} all-reduce(f32[64,64]{0,1:T(8,128)S(1)} %convolution_bitcast_fusion.2), channel_id=1, replica_groups=mesh['rows'=128,'grp'=4] {'rows','grp'}, use_global_device_ids=true, to_apply=%region_14.22 | all-reduce | flops 4096 | bytes 32768 | tf_op jit(solution)/shard_map/psum | solution.py:90
  825.6 5.8 cholesky.55
  832.8 4.9 custom-call.7
  (325 shorter events, 127.4 us)
Async XLA Ops:
  0.6 351.1 %copy-start = (bf16[128,64]{0,1:T(8,128)(2,1)S(1)}, bf16[128,64]{0,1:T(8,128)(2,1)}, u32[]{:S(2)}) copy-start(bf16[128,64]{0,1:T(8,128)(2,1)} %param.30) | copy-start | bytes 49156
  0.6 53.5 %copy-start.1 = (bf16[1,1536,128]{2,1,0:T(8,128)(2,1)S(1)}, bf16[1,1536,128]{2,1,0:T(8,128)(2,1)}, u32[]{:S(2)}) copy-start(bf16[1,1536,128]{2,1,0:T(8,128)(2,1)} %param.25) | copy-start | bytes 1179652
  4.0 35.2 %all-to-all-start = ((s32[128,1,1]{2,1,0:T(1,128)}), s32[128,1,1]{2,1,0:T(1,128)S(1)}, u32[]{:S(2)}, u32[]{:S(2)}) async-start(s32[128,1,1]{2,1,0:T(1,128)} %copy.68), calls=%async_computation | async-start | bytes 131072 | tf_op jit(solution)/shard_map/all_to_all | solution.py:129
  48.5 20.7 %all-to-all-start.2 = ((bf16[128,1,128]{2,1,0:T(2,128)(2,1)}), bf16[128,1,128]{2,1,0:T(2,128)(2,1)S(1)}, u32[]{:S(2)}, u32[]{:S(2)}) async-start(bf16[128,1,128]{2,1,0:T(2,128)(2,1)} %copy.70), calls=%async_computation.2 | async-start | bytes 131072 | tf_op jit(solution)/shard_map/all_to_all | solution.py:134
  61.7 17.2 %copy-start.2 = (s32[1,12]{1,0:T(1,128)S(1)}, s32[1,12]{1,0:T(1,128)}, u32[]{:S(2)}) copy-start(s32[1,12]{1,0:T(1,128)} %param.29) | copy-start | bytes 148
  69.2 192.9 %all-to-all-start.1 = ((bf16[128,1,128,128]{3,2,1,0:T(8,128)(2,1)}), bf16[128,1,128,128]{3,2,1,0:T(8,128)(2,1)}, u32[]{:S(2)}, u32[]{:S(2)}) async-start(bf16[128,1,128,128]{3,2,1,0:T(8,128)(2,1)} %fusion.70), calls=%async_computation.1 | async-start | bytes 8388608 | tf_op jit(solution)/shard_map/all_to_all | solution.py:131
  317.8 28.0 %all-to-all-start.3 = ((bf16[128,1,128]{2,1,0:T(2,128)(2,1)}), bf16[128,1,128]{2,1,0:T(2,128)(2,1)S(1)}, u32[]{:S(2)}, u32[]{:S(2)}) async-start(bf16[128,1,128]{2,1,0:T(2,128)(2,1)} %copy.71), calls=%async_computation.3 | async-start | bytes 131072 | tf_op jit(solution)/shard_map/all_to_all | solution.py:153
  345.7 20.8 %all-to-all-start.4 = ((bf16[128,1,128]{2,1,0:T(2,128)(2,1)}), bf16[128,1,128]{2,1,0:T(2,128)(2,1)S(1)}, u32[]{:S(2)}, u32[]{:S(2)}) async-start(bf16[128,1,128]{2,1,0:T(2,128)(2,1)} %copy.72), calls=%async_computation.4 | async-start | bytes 131072 | tf_op jit(solution)/shard_map/all_to_all | solution.py:137
  558.1 106.2 %all-to-all-start.5 = ((bf16[128,1,64,128]{3,2,1,0:T(8,128)(2,1)}), bf16[128,1,64,128]{3,2,1,0:T(8,128)(2,1)S(1)}, u32[]{:S(2)}, u32[]{:S(2)}) async-start(bf16[128,1,64,128]{3,2,1,0:T(8,128)(2,1)} %fusion.71), calls=%async_computation.5 | async-start | bytes 4194304 | tf_op jit(solution)/shard_map/all_to_all | solution.py:185
where the time goes:
time: 850 us; the launch traced here: 839 us
  waiting for transfers between devices  326 us (38%)
  blocking collectives  203 us (24%)
  local copies, waits for them, and re-layouts  133 us (16%)
  starting transfers between devices  63.9 us (8%)
  other arithmetic  60.4 us (7%)
  matrix products  40 us (5%)
  loops' own time  11.9 us (1%)
    psum x2, blocking collectives, orthonormal(): gram_matrix = lax.psum(local_gram, ('rows', 'grp')) / total_rows  203 us
    all_to_all x1, waiting for transfers between devices, shards(): lax.all_to_all(jnp.take(own_rows, requested, axis=0), 'rows', split_axis=...  182 us
    gather x72, local copies, waits for them, and re-layouts, one_block(): gathered = [jnp.take(member, slot_block, axis=0) for member in pool_arrays]  107 us
    all_to_all x1, waiting for transfers between devices, shards(): lax.all_to_all(jnp.take(own_next, requested, axis=0), 'rows', split_axis=...  93.9 us
    dot_general x12, matrix products, kernel_tiles(): jnp.einsum('naf,nsbf->nsab', own_rows, part_rows, preferred_element_type=...  21.5 us
    all_to_all x1, starting transfers between devices, shards(): lax.all_to_all(wanted, 'rows', split_axis=0, concat_axis=0, tiled=True)  20.4 us
  transfers between devices with their start and end apart: 6, of which 6 were waited for; matrix products, arithmetic and copies ran while one was open for 2% of the time, Pallas kernels for 0%

commit v1 on v0

--- a/solution.py
+++ b/solution.py
@@ -87,7 +87,7 @@
 
 def orthonormal(raw_basis, total_rows):
     local_gram = jnp.einsum("nca,nda->cd", raw_basis, raw_basis, precision=lax.Precision.HIGHEST)
-    gram_matrix = lax.psum(local_gram, ("rows", "grp")) / total_rows
+    gram_matrix = lax.psum(lax.psum(local_gram, "rows"), "grp") / total_rows
     lower = jnp.linalg.cholesky(gram_matrix)
     identity = jnp.eye(gram_matrix.shape[0], dtype=jnp.float32)
     lower_inverse = lax.linalg.triangular_solve(lower, identity, left_side=True, lower=True)

time: 850 us -> 1660 us (1.95)
  blocking collectives: 203 us -> 999 us
    psum x2 -> x4, blocking collectives: 203 us -> 999 us  [orthonormal(): gram_matrix = lax.psum(lax.psum(local_gram, 'rows'), 'grp') / total_rows]
  transfers between devices with their start and end apart: 6 -> 6, of which waited for: 6 -> 6; matrix products, arithmetic and copies ran while one was open for 2% -> 1% of each run, Pallas kernels for 0% -> 0%
where the time goes in v1:
time: 1660 us; the launch traced here: 1640 us
  blocking collectives  999 us (60%)
  waiting for transfers between devices  326 us (20%)
  local copies, waits for them, and re-layouts  133 us (8%)
  starting transfers between devices  70.3 us (4%)
  other arithmetic  60.5 us (4%)
  matrix products  39.9 us (2%)
    psum x4, blocking collectives, orthonormal(): gram_matrix = lax.psum(lax.psum(local_gram, 'rows'), 'grp') / total_rows  999 us
    all_to_all x1, waiting for transfers between devices, shards(): lax.all_to_all(jnp.take(own_rows, requested, axis=0), 'rows', split_axis=...  182 us
    gather x72, local copies, waits for them, and re-layouts, one_block(): gathered = [jnp.take(member, slot_block, axis=0) for member in pool_arrays]  107 us
    all_to_all x1, waiting for transfers between devices, shards(): lax.all_to_all(jnp.take(own_next, requested, axis=0), 'rows', split_axis=...  93.9 us
  transfers between devices with their start and end apart: 6, of which 6 were waited for; matrix products, arithmetic and copies ran while one was open for 1% of the time, Pallas kernels for 0%

profile of v1, /device:TPU:1, one launch (start us, length us, event | category | flops | bytes accessed | tf_op | source)
XLA Modules:
  0.0 1641.9 jit_solution(17180399961264426176)
XLA Ops:
  4.0 20.4 %all-to-all-start = ((s32[128,1,1]{2,1,0:T(1,128)}), s32[128,1,1]{2,1,0:T(1,128)S(1)}, u32[]{:S(2)}, u32[]{:S(2)}) async-start(s32[128,1,1]{2,1,0:T(1,128)} %copy.68), calls=%async_computation | async-start | bytes 131072 | tf_op jit(solution)/shard_map/all_to_all | solution.py:129
  25.8 13.4 all-to-all-done
  41.6 2.4 and_reduce_fusion
  43.9 2.4 reduce.7
  48.5 5.6 all-to-all-start.2
  54.2 3.0 gather_fusion.12
  57.2 4.6 fusion.70
  61.7 7.5 all-to-all-done.2
  69.2 9.3 all-to-all-start.1
  79.7 182.3 %all-to-all-done.1 = bf16[128,1,128,128]{3,2,1,0:T(8,128)(2,1)} async-done(((bf16[128,1,128,128]{3,2,1,0:T(8,128)(2,1)}), bf16[128,1,128,128]{3,2,1,0:T(8,128)(2,1)}, u32[]{:S(2)}, u32[]{:S(2)}) %all-to-all-start.1) | async-done | bytes 4194336 | tf_op jit(solution)/shard_map/all_to_all | solution.py:131
  262.1 4.6 pad_maximum_fusion
  266.7 4.4 fusion.69
  271.2 45.2 %while.32 = (s32[]{:T(128)}, f32[6,2,128]{2,1,0:T(2,128)S(1)}, s32[6]{0:T(128)S(1)}, pred[12,16]{1,0:T(8,128)(4,1)S(1)}, f32[12,128]{1,0:T(8,128)S(1)}, /*index=...) while((s32[]{:T(128)}, f32[6,2,128]{2,1,0:T(2,128)S(1)}, ...), condition=%wide.region_5.10_spmd, body=%wide.region_3.9_spmd.sunk | while | flops 139474112 | bytes 3365755 | solution.py:61
  273.8 3.0 gather_fusion
  281.3 3.0 gather_fusion
  288.8 3.0 gather_fusion
  296.4 3.0 gather_fusion
  303.9 3.0 gather_fusion
  311.4 3.0 gather_fusion
  317.8 13.1 all-to-all-start.3
  331.0 14.8 all-to-all-done.3
  345.8 6.2 all-to-all-start.4
  352.4 14.5 all-to-all-done.4
  367.0 3.8 fusion.72
  372.4 69.3 %while.33 = (s32[]{:T(128)}, f32[6,2,128]{2,1,0:T(2,128)S(1)}, f32[6,2,64,128]{3,2,1,0:T(8,128)S(1)}, s32[6]{0:T(128)S(1)}, pred[12,16]{1,0:T(8,128)(4,1)S(1)}, ...) while((s32[]{:T(128)}, f32[6,2,128]{2,1,0:T(2,128)S(1)}, ...), condition=%wide.region_8.14_spmd, body=%wide.region_6.13_spmd.sunk | while | flops 208422080 | bytes 8232599 | solution.py:61
  375.7 3.0 gather_fusion.3
  387.2 3.0 gather_fusion.3
  398.8 3.0 gather_fusion.3
  410.3 3.0 gather_fusion.3
  421.9 3.0 gather_fusion.3
  433.4 3.0 gather_fusion.3
  442.2 486.5 %psum.28 = f32[64,64]{0,1:T(8,128)S(1)} all-reduce(f32[64,64]{0,1:T(8,128)S(1)} %convolution_bitcast_fusion.4), channel_id=1, replica_groups=mesh['rows'=128,'grp'=4] {'rows'}, use_global_device_ids=true, to_apply=%region_9.15 | all-reduce | flops 4096 | bytes 32768 | tf_op jit(solution)/shard_map/psum | solution.py:90
  928.7 13.7 psum.29
  942.5 5.8 cholesky.44
  949.7 4.9 custom-call.6
  958.0 15.6 all-to-all-start.5
  976.5 93.9 %all-to-all-done.5 = bf16[128,1,64,128]{3,2,1,0:T(8,128)(2,1)S(1)} async-done(((bf16[128,1,64,128]{3,2,1,0:T(8,128)(2,1)}), bf16[128,1,64,128]{3,2,1,0:T(8,128)(2,1)S(1)}, u32[]{:S(2)}, u32[]{:S(2)}) %all-to-all-start.5) | async-done | bytes 2097184 | tf_op jit(solution)/shard_map/all_to_all | solution.py:185
  1072.0 57.1 %while.34 = (s32[]{:T(128)}, f32[6,2,64,128]{3,2,1,0:T(8,128)S(1)}, s32[6]{0:T(128)S(1)}, s32[12,16]{1,0:T(8,128)S(1)}, bf16[140,64,128]{2,1,0:T(8,128)(2,1)}, /...) while((s32[]{:T(128)}, f32[6,2,64,128]{3,2,1,0:T(8,128)S(1)}, ...), condition=%wide.region_14.22_spmd, body=%wide.region_13.21_spmd.sunk | while | flops 206845376 | bytes 5001731 | solution.py:61
  1074.6 3.0 gather_fusion.8
  1084.1 3.0 gather_fusion.8
  1093.6 3.0 gather_fusion.8
  1103.2 3.0 gather_fusion.8
  1112.7 3.0 gather_fusion.8
  1122.2 3.0 gather_fusion.8
  1129.6 487.5 %psum.30 = f32[64,64]{0,1:T(8,128)S(1)} all-reduce(f32[64,64]{0,1:T(8,128)S(1)} %convolution_bitcast_fusion.2), channel_id=1, replica_groups=mesh['rows'=128,'grp'=4] {'rows'}, use_global_device_ids=true, to_apply=%region_15.23 | all-reduce | flops 4096 | bytes 32768 | tf_op jit(solution)/shard_map/psum | solution.py:90
  1617.1 10.9 psum.31
  1628.1 5.8 cholesky.55
  1635.3 4.9 custom-call.7
  (327 shorter events, 132.0 us)
Async XLA Ops:
  0.6 351.4 %copy-start = (bf16[128,64]{0,1:T(8,128)(2,1)S(1)}, bf16[128,64]{0,1:T(8,128)(2,1)}, u32[]{:S(2)}) copy-start(bf16[128,64]{0,1:T(8,128)(2,1)} %param.30) | copy-start | bytes 49156
  0.6 53.5 %copy-start.1 = (bf16[1,1536,128]{2,1,0:T(8,128)(2,1)S(1)}, bf16[1,1536,128]{2,1,0:T(8,128)(2,1)}, u32[]{:S(2)}) copy-start(bf16[1,1536,128]{2,1,0:T(8,128)(2,1)} %param.25) | copy-start | bytes 1179652
  4.0 35.2 %all-to-all-start = ((s32[128,1,1]{2,1,0:T(1,128)}), s32[128,1,1]{2,1,0:T(1,128)S(1)}, u32[]{:S(2)}, u32[]{:S(2)}) async-start(s32[128,1,1]{2,1,0:T(1,128)} %copy.68), calls=%async_computation | async-start | bytes 131072 | tf_op jit(solution)/shard_map/all_to_all | solution.py:129
  48.5 20.7 %all-to-all-start.2 = ((bf16[128,1,128]{2,1,0:T(2,128)(2,1)}), bf16[128,1,128]{2,1,0:T(2,128)(2,1)S(1)}, u32[]{:S(2)}, u32[]{:S(2)}) async-start(bf16[128,1,128]{2,1,0:T(2,128)(2,1)} %copy.70), calls=%async_computation.2 | async-start | bytes 131072 | tf_op jit(solution)/shard_map/all_to_all | solution.py:134
  61.7 17.2 %copy-start.2 = (s32[1,12]{1,0:T(1,128)S(1)}, s32[1,12]{1,0:T(1,128)}, u32[]{:S(2)}) copy-start(s32[1,12]{1,0:T(1,128)} %param.29) | copy-start | bytes 148
  69.2 192.9 %all-to-all-start.1 = ((bf16[128,1,128,128]{3,2,1,0:T(8,128)(2,1)}), bf16[128,1,128,128]{3,2,1,0:T(8,128)(2,1)}, u32[]{:S(2)}, u32[]{:S(2)}) async-start(bf16[128,1,128,128]{3,2,1,0:T(8,128)(2,1)} %fusion.70), calls=%async_computation.1 | async-start | bytes 8388608 | tf_op jit(solution)/shard_map/all_to_all | solution.py:131
  317.8 28.0 %all-to-all-start.3 = ((bf16[128,1,128]{2,1,0:T(2,128)(2,1)}), bf16[128,1,128]{2,1,0:T(2,128)(2,1)S(1)}, u32[]{:S(2)}, u32[]{:S(2)}) async-start(bf16[128,1,128]{2,1,0:T(2,128)(2,1)} %copy.71), calls=%async_computation.3 | async-start | bytes 131072 | tf_op jit(solution)/shard_map/all_to_all | solution.py:153
  345.8 21.1 %all-to-all-start.4 = ((bf16[128,1,128]{2,1,0:T(2,128)(2,1)}), bf16[128,1,128]{2,1,0:T(2,128)(2,1)S(1)}, u32[]{:S(2)}, u32[]{:S(2)}) async-start(bf16[128,1,128]{2,1,0:T(2,128)(2,1)} %copy.72), calls=%async_computation.4 | async-start | bytes 131072 | tf_op jit(solution)/shard_map/all_to_all | solution.py:137
  958.0 112.3 %all-to-all-start.5 = ((bf16[128,1,64,128]{3,2,1,0:T(8,128)(2,1)}), bf16[128,1,64,128]{3,2,1,0:T(8,128)(2,1)S(1)}, u32[]{:S(2)}, u32[]{:S(2)}) async-start(bf16[128,1,64,128]{3,2,1,0:T(8,128)(2,1)} %fusion.71), calls=%async_computation.5 | async-start | bytes 4194304 | tf_op jit(solution)/shard_map/all_to_all | solution.py:185
